TPU v7x, 32 devices: a whole 2x2x4 slice. The times are simulated.
32 devices in a mesh: grp: 4 (over y, core), dev: 8 (over z, x).
Axes of the slice: x: 2, y: 2, z: 4, core: 2. Of those that a mesh axis runs over, the one named last changes fastest.
Arguments:
- densities: bfloat16 [32, 200, 200], P(('grp', 'dev')), may hold values from -0.4375 to 0.4375
- core_hamiltonian: bfloat16 [32, 200, 200], P(('grp', 'dev')), may hold values from -0.21875 to 0.21875
- embedding: bfloat16 [32, 200, 200], P(('grp', 'dev')), may hold values from -0.21875 to 0.21875
- fit_factors: bfloat16 [192, 200, 200], P('dev'), may hold values from -0.059814453 to 0.059814453
- orthogonalizers: bfloat16 [32, 200, 200], P(('grp', 'dev'))
- pairs: int32 [384, 2], replicated, may hold values from 0 to 31, as said below
- assignment: int32 [384], replicated, may hold values from 0 to 7, as said below
- owner_map: int32 [32], replicated, may hold values from 0 to 31, as said below
Outputs:
- slot_energies: float32 [768], P(('grp', 'dev'))
- total: float32 [], replicated
Inputs may be any that keep to these rules, and one draw needn't show every extreme that they name: `pairs`: dimer k belongs to group g = k // 96; its first fragment lies in block g, the fragments g * 8 to (g + 1) * 8 - 1, and its second fragment, different from the first, lies in block g or block g + 1 (only block g for the last group). `assignment`: no device receives more than 24 dimers of its group, and in every group some device receives exactly 24. `owner_map`: A permutation of the fragments that maps each block of 8 fragments onto the rows of the same block.
All inputs are finite; a program needn't handle non-finite values.
Results may differ from a plain program's by a relative error of at most 0.0003.
Values may be sent and summed in bfloat16 or wider, within the bound.
A program may use at most 128 MiB of HBM per device.

v0:
```python
import jax
import jax.numpy as jnp
from jax import lax
from jax.sharding import PartitionSpec as P

SLOTS = 24
F32 = jnp.float32
BF = jnp.bfloat16


def dot(left, right, dims=((1,), (0,))):
    return lax.dot_general(left, right, (dims, ((), ())), preferred_element_type=F32)


def lookup(table, mono, pairs, assignment, owner_map, group, member, members, groups):
    count = pairs.shape[0]
    per_group = count // groups
    rows = members * groups
    frag_ids = jnp.arange(rows, dtype=jnp.int32)
    row_of = lambda frag: jnp.sum(
        jnp.where(frag[:, None] == frag_ids[None, :], owner_map[None, :], 0), axis=1
    )
    first, second = (row_of(pairs[:, 0]), row_of(pairs[:, 1]))
    column = second - jnp.arange(count, dtype=jnp.int32) // per_group * members
    table_rows = jnp.sum(
        jnp.where((first[:, None] == frag_ids[None, :])[:, :, None], table[None, :, :], 0.0), axis=1
    )
    columns = jnp.arange(2 * members, dtype=jnp.int32)
    energies = jnp.sum(jnp.where(column[:, None] == columns[None, :], table_rows, 0.0), axis=1)
    energies = energies + jnp.sum(
        jnp.where(second[:, None] == frag_ids[None, :], mono[None, :], 0.0), axis=1
    )
    start = group * per_group
    mine = lax.dynamic_slice_in_dim(assignment, start, per_group, 0) == member
    mine_count = mine.astype(jnp.int32)
    before = jnp.cumsum(mine_count) - mine_count
    select = mine[None, :] & (before[None, :] == jnp.arange(SLOTS, dtype=jnp.int32)[:, None])
    own = lax.dynamic_slice_in_dim(energies, start, per_group, 0)
    return (jnp.sum(jnp.where(select, own[None, :], 0.0), axis=1), jnp.sum(energies))


def on_device(dens, core, embed, fit, ortho, pairs, assignment, owner_map):
    members, groups = (lax.axis_size("dev"), lax.axis_size("grp"))
    group, member = (lax.axis_index("grp"), lax.axis_index("dev"))
    basis = dens.shape[1]
    aux = fit.shape[0]
    flat_fit = fit.reshape(aux, basis * basis)
    gathered = lax.all_gather(dens, "dev", axis=0, tiled=True)
    coeffs = dot(gathered.reshape(members, basis * basis), flat_fit, ((1,), (1,))).astype(BF)
    coulomb = lax.psum_scatter(
        dot(coeffs, flat_fit).reshape(members, basis, basis).astype(BF),
        "dev",
        scatter_dimension=0,
        tiled=True,
    ).astype(F32)
    fock = (core.astype(F32) + embed.astype(F32) + coulomb).astype(BF)[0]
    d, x = (dens[0], ortho[0])
    v = dot(fock, x).astype(BF)
    u = dot(d, x).astype(BF)
    xf = dot(x, fock, ((0,), (0,))).astype(BF)
    xd = dot(x, d, ((0,), (0,))).astype(BF)
    a = dot(x, v, ((0,), (0,)))
    a_sym = (0.5 * (a + a.T)).astype(BF)
    ab = a.astype(BF)
    mono = (
        0.5 * jnp.trace(a)
        - 0.1875 * jnp.sum(a * a)
        + jnp.sum(dot(ab, ab) * dot(ab, ab, ((1,), (1,)))) / 256.0
        - jnp.sum(d.astype(F32) * fock.astype(F32))
    )
    block = jnp.stack([u, v, a_sym])[None]
    own_pool = lax.all_gather(block, "dev", axis=0, tiled=True)
    route = [(g, (g - 1) % groups) for g in range(groups)]
    next_pool = lax.ppermute(own_pool, "grp", route)
    pool = jnp.concatenate([own_pool, next_pool], axis=0)

    def pair_term(entry):
        u_j, v_j, c_sym = (entry[0], entry[1], entry[2])
        b = 0.5 * (dot(xf, u_j) + dot(xd, v_j))
        bb = b.astype(BF)
        left, right, gram = (dot(a_sym, bb), dot(bb, c_sym), dot(bb, bb, ((1,), (1,))))
        both = left + right
        quartic = left * left + right * right + both * both + gram * gram
        return jnp.sum(quartic / 128.0 - 0.375 * (b * b))

    terms = lax.map(pair_term, pool)
    line = jnp.concatenate([terms + mono, mono[None]])
    table = lax.all_gather(line[None], ("grp", "dev"), axis=0, tiled=True)
    return lookup(
        table[:, :-1], table[:, -1], pairs, assignment, owner_map, group, member, members, groups
    )


def solution(mesh):
    rows = P(("grp", "dev"), None, None)
    placed = (rows, rows, rows, P("dev", None, None), rows, P(), P(), P())
    return jax.shard_map(
        on_device, mesh=mesh, in_specs=placed, out_specs=(P(("grp", "dev")), P()), check_vma=False
    )
```

profile of v0, /device:TPU:0, one launch (start us, length us, event | category | flops | bytes accessed | tf_op | source)
XLA Modules:
  0.0 337.6 jit_solution(6582617387170707575)
XLA Ops:
  7.2 5.0 %reshape.89 = bf16[24,40000]{1,0:T(8,128)(2,1)} reshape(bf16[24,200,200]{2,1,0:T(8,128)(2,1)} %param.13) | data formatting | bytes 3840000 | tf_op jit(solution)/shard_map/reshape | solution.py:47
  12.2 6.2 %dot_general.53 = bf16[200,200,24]{1,0,2:T(8,128)(2,1)} reshape(bf16[40000,24]{0,1:T(8,128)(2,1)} %bitcast.123) | data formatting | bytes 3840000 | tf_op jit(solution)/shard_map/dot_general | solution.py:12
  18.4 36.1 %all_gather.9 = bf16[8,200,200]{2,1,0:T(8,128)(2,1)} all-gather(bf16[1,200,200]{2,1,0:T(8,128)(2,1)S(1)} %copy-done.2), channel_id=1, replica_groups=mesh['grp'=4,'dev'=8] {'dev'}, dimensions={0}, use_global_device_ids=true | all-gather | bytes 720000 | tf_op jit(solution)/shard_map/all_gather | solution.py:48
  54.5 3.9 %fusion.17 = bf16[8,200,200]{2,0,1:T(8,128)(2,1)S(1)} fusion(bf16[200,200,24]{1,0,2:T(8,128)(2,1)} %dot_general.53, bf16[24,200,200]{2,1,0:T(8,128)(2,1)S(1)} %copy-done.1, bf16[8,200,200]{2,1,0:T(8,128)(2,1)} %all_gather.9), kind=kOutput, calls=%fused_computation.24 | convolution fusion | flops 31040192 | bytes 5120000 | tf_op jit(solution)/shard_map/dot_general | solution.py:12
  58.4 1.0 copy.66
  59.7 58.7 %reduce-scatter.2.cloned.1.call-done = bf16[1,200,200]{2,1,0:T(8,128)(2,1)} async-done(((bf16[8,200,200]{2,1,0:T(8,128)(2,1)}), bf16[1,200,200]{2,1,0:T(8,128)(2,1)}) %reduce-scatter.2.cloned.1.call-update) | async-done | bytes 80016 | tf_op jit(solution)/shard_map/reduce_scatter | solution.py:50
  118.4 1.6 multiply_reduce_fusion
  122.0 52.0 %all-gather.4.cloned.1.call-done = bf16[24,200,200]{2,1,0:T(8,128)(2,1)} async-done(((bf16[3,200,200]{2,1,0:T(8,128)(2,1)}), bf16[24,200,200]{2,1,0:T(8,128)(2,1)}) %all-gather.4.cloned.1.call-update) | async-done | bytes 1920016 | tf_op jit(solution)/shard_map/all_gather | solution.py:72
  179.5 22.2 %collective-permute-done = bf16[8,3,200,200]{3,2,1,0:T(8,128)(2,1)S(1)} collective-permute-done((bf16[8,3,200,200]{3,2,1,0:T(8,128)(2,1)}, bf16[8,3,200,200]{3,2,1,0:T(8,128)(2,1)S(1)}, u32[]{:S(2)}, u32[]{:S(2)}) %collective-permute-start) | collective-permute-done | bytes 1920032 | tf_op jit(solution)/shard_map/ppermute | solution.py:74
  201.7 4.7 %pad_maximum_fusion = bf16[16,3,200,200]{3,2,1,0:T(8,128)(2,1)} fusion(bf16[8,3,200,200]{3,2,1,0:T(8,128)(2,1)S(1)} %collective-permute-done, bf16[8,3,200,200]{3,2,1,0:T(8,128)(2,1)} %bitcast.126), kind=kLoop, calls=%fused_computation.19 | loop fusion | flops 1920000 | bytes 7680000 | tf_op jit(solution)/shard_map/concatenate | solution.py:75
  206.4 82.9 %while.10 = (s32[]{:T(128)}, f32[16]{0:T(128)S(1)}, bf16[16,3,200,200]{3,2,1,0:T(8,128)(2,1)}, bf16[200,200]{1,0:T(8,128)(2,1)S(1)}, bf16[200,200]{1,0:T(8,128)(...) while((s32[]{:T(128)}, f32[16]{0:T(128)S(1)}, ...), condition=%wide.region_6.7_spmd, body=%wide.region_4.6_spmd.sunk | while | flops 80720000 | bytes 2147369 | solution.py:86
  206.4 1.1 fusion.93
  207.5 1.1 fusion.94
  208.9 1.1 fusion.95
  211.6 1.1 fusion.93
  212.7 1.1 fusion.94
  214.0 1.1 fusion.95
  215.2 0.8 fusion.96
  216.8 1.1 fusion.93
  217.9 1.1 fusion.94
  219.2 1.1 fusion.95
  220.4 0.8 fusion.96
  222.0 1.1 fusion.93
  223.1 1.1 fusion.94
  224.4 1.1 fusion.95
  227.2 1.1 fusion.93
  228.3 1.1 fusion.94
  229.6 1.1 fusion.95
  230.7 0.8 fusion.96
  232.3 1.1 fusion.93
  233.5 1.1 fusion.94
  234.8 1.1 fusion.95
  237.5 1.1 fusion.93
  238.6 1.1 fusion.94
  240.0 1.1 fusion.95
  242.7 1.1 fusion.93
  243.8 1.1 fusion.94
  245.2 1.1 fusion.95
  247.9 1.1 fusion.93
  249.0 1.1 fusion.94
  250.3 1.1 fusion.95
  253.1 1.1 fusion.93
  254.2 1.1 fusion.94
  255.5 1.1 fusion.95
  258.3 1.1 fusion.93
  259.4 1.1 fusion.94
  260.7 1.1 fusion.95
  263.4 1.1 fusion.93
  264.6 1.1 fusion.94
  265.9 1.1 fusion.95
  268.6 1.1 fusion.93
  269.7 1.1 fusion.94
  271.1 1.1 fusion.95
  273.8 1.1 fusion.93
  274.9 1.1 fusion.94
  276.2 1.1 fusion.95
  279.0 1.1 fusion.93
  280.1 1.1 fusion.94
  281.4 1.1 fusion.95
  282.6 0.8 fusion.96
  284.2 1.1 fusion.93
  285.3 1.1 fusion.94
  286.6 1.1 fusion.95
  289.5 39.4 %all-reduce = f32[544]{0:T(1024)S(1)} all-reduce(f32[544]{0:T(1024)S(1)} %maximum_dynamic-update-slice_fusion), channel_id=3, replica_groups=mesh['grp'=4,'dev'=8] {'grp','dev'}, use_global_device_ids=true, to_apply=%add | all-reduce | flops 544 | bytes 4352
  (97 shorter events, 32.6 us)
Async XLA Ops:
  7.2 52.4 %copy-start = (bf16[1,200,200]{2,1,0:T(8,128)(2,1)S(1)}, bf16[1,200,200]{2,1,0:T(8,128)(2,1)}, u32[]{:S(2)}) copy-start(bf16[1,200,200]{2,1,0:T(8,128)(2,1)} %param.14) | copy-start | bytes 240004
  7.2 111.2 %reduce-scatter.2.cloned.1.call-start = ((), (), s32[]{:S(2)}) async-start(), calls=%async_computation.1 | async-start | bytes 921600 | tf_op jit(solution)/shard_map/reduce_scatter | solution.py:50
  12.2 6.2 %copy-start.2 = (bf16[1,200,200]{2,1,0:T(8,128)(2,1)S(1)}, bf16[1,200,200]{2,1,0:T(8,128)(2,1)}, u32[]{:S(2)}) copy-start(bf16[1,200,200]{2,1,0:T(8,128)(2,1)} %param.10) | copy-start | bytes 240004
  12.2 42.3 %copy-start.1 = (bf16[24,200,200]{2,1,0:T(8,128)(2,1)S(1)}, bf16[24,200,200]{2,1,0:T(8,128)(2,1)}, u32[]{:S(2)}) copy-start(bf16[24,200,200]{2,1,0:T(8,128)(2,1)} %param.13) | copy-start | bytes 5760004
  58.4 60.1 %copy-start.4 = (bf16[1,200,200]{2,1,0:T(8,128)(2,1)S(1)}, bf16[1,200,200]{2,1,0:T(8,128)(2,1)}, u32[]{:S(2)}) copy-start(bf16[1,200,200]{2,1,0:T(8,128)(2,1)} %param.12) | copy-start | bytes 240004
  58.4 60.0 %copy-start.5 = (bf16[1,200,200]{2,1,0:T(8,128)(2,1)S(1)}, bf16[1,200,200]{2,1,0:T(8,128)(2,1)}, u32[]{:S(2)}) copy-start(bf16[1,200,200]{2,1,0:T(8,128)(2,1)} %param.11) | copy-start | bytes 240004
  59.4 115.7 %copy-start.6 = (s32[384,2]{0,1:T(2,128)S(1)}, s32[384,2]{0,1:T(2,128)}, u32[]{:S(2)}) copy-start(s32[384,2]{0,1:T(2,128)} %param.15) | copy-start | bytes 9220
  59.4 115.7 %copy-start.7 = (s32[32]{0:T(128)S(1)}, s32[32]{0:T(128)}, u32[]{:S(2)}) copy-start(s32[32]{0:T(128)} %param.17) | copy-start | bytes 388
  59.5 115.9 %copy-start.3 = (bf16[1,200,200]{2,1,0:T(8,128)(2,1)S(1)}, bf16[1,200,200]{2,1,0:T(8,128)(2,1)}, u32[]{:S(2)}) copy-start(bf16[1,200,200]{2,1,0:T(8,128)(2,1)} %param.10) | copy-start | bytes 240004
  59.5 114.5 %all-gather.4.cloned.1.call-start = ((), (), s32[]{:S(2)}) async-start(), calls=%async_computation.2 | async-start | bytes 2764800 | tf_op jit(solution)/shard_map/all_gather | solution.py:72
  174.0 27.7 %collective-permute-start = (bf16[8,3,200,200]{3,2,1,0:T(8,128)(2,1)}, bf16[8,3,200,200]{3,2,1,0:T(8,128)(2,1)S(1)}, u32[]{:S(2)}, u32[]{:S(2)}) collective-permute-start(bf16[8,3,200,200]{3,2,1,0:T(8,128)(2,1)} %bitcast.125), channel_id=1, source_target_pairs={{0,24},{8,0},{16,8},{24,16},{1,25},{9,1},{17,9},{25,17},{2,26},{10... | collective-permute-start | bytes 5760008 | tf_op jit(solution)/shard_map/ppermute | solution.py:74
Sparse Core Ops, SparseCore 0:
  59.6 58.7 reduce-scatter.1
  122.2 51.7 all-gather.3
where the time goes:
time: 340 us; the launch traced here: 338 us
  waiting for transfers between devices  133 us (39%)
  matrix products  76.3 us (22%)
  blocking collectives  75.5 us (22%)
  local copies, waits for them, and re-layouts  25 us (7%)
  between operations  16.9 us (5%)
  other arithmetic  10.5 us (3%)
    dot_general x88, matrix products, dot(): lax.dot_general(left, right, (dims, ((), ())), preferred_element_type=F32)  76.3 us
    reduce_scatter x1, waiting for transfers between devices, on_device(): lax.psum_scatter(dot(coeffs, flat_fit).reshape(members, basis, basis).ast...  58.7 us
    all_gather x1, waiting for transfers between devices, on_device(): own_pool = lax.all_gather(block, 'dev', axis=0, tiled=True)  52 us
    unnamed x1, blocking collectives  39.4 us
    all_gather x1, blocking collectives, on_device(): gathered = lax.all_gather(dens, 'dev', axis=0, tiled=True)  36.1 us
    ppermute x1, waiting for transfers between devices, on_device(): next_pool = lax.ppermute(own_pool, 'grp', route)  22.2 us
    dynamic_update_slice x16, local copies, waits for them, and re-layouts, on_device(): terms = lax.map(pair_term, pool)  12.1 us
  transfers between devices with their start and end apart: 3, of which 3 were waited for; matrix products, arithmetic and copies ran while one was open for 1% of the time, Pallas kernels for 0%

commit v1 on v0

--- a/solution.py
+++ b/solution.py
@@ -1,3 +1,4 @@
+import functools
 import jax
 import jax.numpy as jnp
 from jax import lax
@@ -6,6 +7,22 @@
 SLOTS = 24
 F32 = jnp.float32
 BF = jnp.bfloat16
+
+
+def define_cube(base_x, mesh_ax):
+    n_axis = lax.axis_size(mesh_ax)
+    heap = [(ii, (ii + 1) % n_axis) for ii in range(n_axis)]
+
+    def state_fields(high):
+        if len(high) == n_axis:
+            return high
+        return state_fields([lax.ppermute(high[0], axis_name=mesh_ax, perm=heap), *high])
+
+    new = jnp.concatenate(state_fields([base_x]), axis=0)
+    return jnp.roll(new, shift=(lax.axis_index(mesh_ax) + 1) * base_x.shape[0], axis=0)
+
+
+counts_report = functools.partial(define_cube, mesh_ax="dev")
 
 
 def dot(left, right, dims=((1,), (0,))):
@@ -45,7 +62,7 @@
     basis = dens.shape[1]
     aux = fit.shape[0]
     flat_fit = fit.reshape(aux, basis * basis)
-    gathered = lax.all_gather(dens, "dev", axis=0, tiled=True)
+    gathered = counts_report(dens)
     coeffs = dot(gathered.reshape(members, basis * basis), flat_fit, ((1,), (1,))).astype(BF)
     coulomb = lax.psum_scatter(
         dot(coeffs, flat_fit).reshape(members, basis, basis).astype(BF),

time: 340 us -> 370 us (1.088)
  waiting for transfers between devices: 133 us -> 185 us
  blocking collectives: 75.5 us -> 39.4 us
  local copies, waits for them, and re-layouts: 25 us -> 35.7 us
    ppermute x0 -> x7, waiting for transfers between devices: none -> 51.9 us  [state_fields(): lax.ppermute(high[0], axis_name=mesh_ax, perm=heap)]
    all_gather x1 -> x0, blocking collectives: 36.1 us -> none  [on_device(): gathered = lax.all_gather(dens, 'dev', axis=0, tiled=True)]
    concatenate x0 -> x1, local copies, waits for them, and re-layouts: none -> 11.1 us  [define_cube(): jnp.roll(new, shift=(lax.axis_index(mesh_ax) + 1) * base_x.shape[0], axis=0)]
  transfers between devices with their start and end apart: 3 -> 10, of which waited for: 3 -> 9; matrix products, arithmetic and copies ran while one was open for 1% -> 3% of each run, Pallas kernels for 0% -> 0%
where the time goes in v1:
time: 370 us; the launch traced here: 368 us
  waiting for transfers between devices  185 us (50%)
  matrix products  76.6 us (21%)
  blocking collectives  39.4 us (11%)
  local copies, waits for them, and re-layouts  35.7 us (10%)
  between operations  16.9 us (5%)
  other arithmetic  10.6 us (3%)
    dot_general x88, matrix products, dot(): lax.dot_general(left, right, (dims, ((), ())), preferred_element_type=F32)  76.6 us
    reduce_scatter x1, waiting for transfers between devices, on_device(): lax.psum_scatter(dot(coeffs, flat_fit).reshape(members, basis, basis).ast...  59.3 us
    all_gather x1, waiting for transfers between devices, on_device(): own_pool = lax.all_gather(block, 'dev', axis=0, tiled=True)  52 us
    ppermute x7, waiting for transfers between devices, state_fields(): lax.ppermute(high[0], axis_name=mesh_ax, perm=heap)  51.9 us
    unnamed x1, blocking collectives  39.4 us
    ppermute x1, waiting for transfers between devices, on_device(): next_pool = lax.ppermute(own_pool, 'grp', route)  22.2 us
    dynamic_update_slice x16, local copies, waits for them, and re-layouts, on_device(): terms = lax.map(pair_term, pool)  12.1 us
    concatenate x1, local copies, waits for them, and re-layouts, define_cube(): jnp.roll(new, shift=(lax.axis_index(mesh_ax) + 1) * base_x.shape[0], axis=0)  11.1 us
  transfers between devices with their start and end apart: 10, of which 9 were waited for; matrix products, arithmetic and copies ran while one was open for 3% of the time, Pallas kernels for 0%

profile of v1, /device:TPU:0, one launch (start us, length us, event | category | flops | bytes accessed | tf_op | source)
XLA Modules:
  0.0 368.0 jit_solution(4242649312820011897)
XLA Ops:
  8.3 3.0 collective-permute-start
  11.3 8.1 %collective-permute-done = bf16[1,200,200]{2,0,1:T(2,128)(2,1)S(1)} collective-permute-done((bf16[1,200,200]{2,0,1:T(2,128)(2,1)S(1)}, bf16[1,200,200]{2,0,1:T(2,128)(2,1)S(1)}, u32[]{:S(2)}, u32[]{:S(2)}) %collective-permute-start) | collective-permute-done | bytes 80032 | tf_op jit(solution)/shard_map/ppermute | solution.py:19
  19.4 8.9 %collective-permute-done.1 = bf16[1,200,200]{2,0,1:T(2,128)(2,1)S(1)} collective-permute-done((bf16[1,200,200]{2,0,1:T(2,128)(2,1)S(1)}, bf16[1,200,200]{2,0,1:T(2,128)(2,1)S(1)}, u32[]{:S(2)}, u32[]{:S(2)}) %collective-permute-start.1) | collective-permute-done | bytes 80032 | tf_op jit(solution)/shard_map/ppermute | solution.py:19
  28.4 8.5 %collective-permute-done.2 = bf16[1,200,200]{2,0,1:T(2,128)(2,1)S(1)} collective-permute-done((bf16[1,200,200]{2,0,1:T(2,128)(2,1)S(1)}, bf16[1,200,200]{2,0,1:T(2,128)(2,1)S(1)}, u32[]{:S(2)}, u32[]{:S(2)}) %collective-permute-start.2) | collective-permute-done | bytes 80032 | tf_op jit(solution)/shard_map/ppermute | solution.py:19
  36.8 8.6 %collective-permute-done.3 = bf16[1,200,200]{2,0,1:T(2,128)(2,1)} collective-permute-done((bf16[1,200,200]{2,0,1:T(2,128)(2,1)S(1)}, bf16[1,200,200]{2,0,1:T(2,128)(2,1)}, u32[]{:S(2)}, u32[]{:S(2)}) %collective-permute-start.3) | collective-permute-done | bytes 80032 | tf_op jit(solution)/shard_map/ppermute | solution.py:19
  45.4 8.7 %collective-permute-done.4 = bf16[1,200,200]{2,0,1:T(2,128)(2,1)S(1)} collective-permute-done((bf16[1,200,200]{2,0,1:T(2,128)(2,1)}, bf16[1,200,200]{2,0,1:T(2,128)(2,1)S(1)}, u32[]{:S(2)}, u32[]{:S(2)}) %collective-permute-start.4) | collective-permute-done | bytes 80032 | tf_op jit(solution)/shard_map/ppermute | solution.py:19
  54.7 9.1 %collective-permute-done.5 = bf16[1,200,200]{2,0,1:T(2,128)(2,1)} collective-permute-done((bf16[1,200,200]{2,0,1:T(2,128)(2,1)S(1)}, bf16[1,200,200]{2,0,1:T(2,128)(2,1)}, u32[]{:S(2)}, u32[]{:S(2)}) %collective-permute-start.5) | collective-permute-done | bytes 80032 | tf_op jit(solution)/shard_map/ppermute | solution.py:19
  63.9 3.9 %reshape.89 = bf16[24,40000]{1,0:T(8,128)(2,1)S(1)} reshape(bf16[24,200,200]{2,1,0:T(8,128)(2,1)} %param.13) | data formatting | bytes 3840000 | tf_op jit(solution)/shard_map/reshape | solution.py:64
  67.8 5.0 %dot_general.53 = bf16[200,200,24]{1,0,2:T(8,128)(2,1)} reshape(bf16[40000,24]{0,1:T(8,128)(2,1)S(1)} %bitcast.123) | data formatting | bytes 3840000 | tf_op jit(solution)/shard_map/dot_general | solution.py:29
  72.8 11.1 %concatenate.12 = bf16[16,200,200]{2,0,1:T(8,128)(2,1)} concatenate(bf16[1,200,200]{2,0,1:T(2,128)(2,1)} %collective-permute-done.6, bf16[1,200,200]{2,0,1:T(2,128)(2,1)} %collective-permute-done.5, bf16[1,200,200]{2,0,1:T(2,128)(2,1)} %copy-done.3, bf16[1,200,200]{2,0,1:T(2,128)(2,1)} %collective-permute-done.3, bf16[1,200,200]{2,0,1:T(2,128)(2,1)S(1)} %collective-permute-done.2, ...), dimensions={0} | concatenate | bytes 2560000 | tf_op jit(solution)/shard_map/jit(_roll_dynamic)/concatenate | solution.py:22
  84.0 4.1 %fusion.17 = bf16[8,200,200]{2,0,1:T(8,128)(2,1)S(1)} fusion(bf16[200,200,24]{1,0,2:T(8,128)(2,1)} %dot_general.53, bf16[24,200,200]{2,1,0:T(8,128)(2,1)S(1)} %copy-done.1, bf16[16,200,200]{2,0,1:T(8,128)(2,1)} %concatenate.12, s32[]{:T(128)S(6)} %select_n.59), kind=kOutput, calls=%fused_computation.24 | convolution fusion | flops 31040192 | bytes 5836804 | tf_op jit(solution)/shard_map/dot_general | solution.py:29
  89.5 59.3 %reduce-scatter.2.cloned.1.call-done = bf16[1,200,200]{2,1,0:T(8,128)(2,1)} async-done(((bf16[8,200,200]{2,1,0:T(8,128)(2,1)}), bf16[1,200,200]{2,1,0:T(8,128)(2,1)}) %reduce-scatter.2.cloned.1.call-update) | async-done | bytes 80016 | tf_op jit(solution)/shard_map/reduce_scatter | solution.py:67
  148.8 1.6 multiply_reduce_fusion
  152.4 52.0 %all-gather.4.cloned.1.call-done = bf16[24,200,200]{2,1,0:T(8,128)(2,1)} async-done(((bf16[3,200,200]{2,1,0:T(8,128)(2,1)}), bf16[24,200,200]{2,1,0:T(8,128)(2,1)}) %all-gather.4.cloned.1.call-update) | async-done | bytes 1920016 | tf_op jit(solution)/shard_map/all_gather | solution.py:89
  209.9 22.2 %collective-permute-done.7 = bf16[8,3,200,200]{3,2,1,0:T(8,128)(2,1)S(1)} collective-permute-done((bf16[8,3,200,200]{3,2,1,0:T(8,128)(2,1)}, bf16[8,3,200,200]{3,2,1,0:T(8,128)(2,1)S(1)}, u32[]{:S(2)}, u32[]{:S(2)}) %collective-permute-start.7) | collective-permute-done | bytes 1920032 | tf_op jit(solution)/shard_map/ppermute | solution.py:91
  232.1 4.7 %pad_maximum_fusion = bf16[16,3,200,200]{3,2,1,0:T(8,128)(2,1)} fusion(bf16[8,3,200,200]{3,2,1,0:T(8,128)(2,1)S(1)} %collective-permute-done.7, bf16[8,3,200,200]{3,2,1,0:T(8,128)(2,1)} %bitcast.126), kind=kLoop, calls=%fused_computation.19 | loop fusion | flops 1920000 | bytes 7680000 | tf_op jit(solution)/shard_map/concatenate | solution.py:92
  236.8 82.9 %while.10 = (s32[]{:T(128)}, f32[16]{0:T(128)S(1)}, bf16[16,3,200,200]{3,2,1,0:T(8,128)(2,1)}, bf16[200,200]{1,0:T(8,128)(2,1)S(1)}, bf16[200,200]{1,0:T(8,128)(...) while((s32[]{:T(128)}, f32[16]{0:T(128)S(1)}, ...), condition=%wide.region_6.7_spmd, body=%wide.region_4.6_spmd.sunk | while | flops 80720000 | bytes 2147369 | solution.py:103
  237.9 1.1 fusion.96
  239.2 1.1 fusion.97
  242.0 1.1 fusion.95
  243.1 1.1 fusion.96
  244.4 1.1 fusion.97
  247.1 1.1 fusion.95
  248.3 1.1 fusion.96
  249.6 1.1 fusion.97
  252.3 1.1 fusion.95
  253.4 1.1 fusion.96
  254.8 1.1 fusion.97
  257.5 1.1 fusion.95
  258.6 1.1 fusion.96
  259.9 1.1 fusion.97
  262.7 1.1 fusion.95
  263.8 1.1 fusion.96
  265.1 1.1 fusion.97
  267.9 1.1 fusion.95
  269.0 1.1 fusion.96
  270.3 1.1 fusion.97
  273.1 1.1 fusion.95
  274.2 1.1 fusion.96
  275.5 1.1 fusion.97
  278.2 1.1 fusion.95
  279.3 1.1 fusion.96
  280.7 1.1 fusion.97
  283.4 1.1 fusion.95
  284.5 1.1 fusion.96
  285.9 1.1 fusion.97
  289.7 1.1 fusion.96
  291.0 1.1 fusion.97
  293.8 1.1 fusion.95
  294.9 1.1 fusion.96
  296.2 1.1 fusion.97
  299.0 1.1 fusion.95
  300.1 1.1 fusion.96
  301.4 1.1 fusion.97
  304.1 1.1 fusion.95
  305.3 1.1 fusion.96
  306.6 1.1 fusion.97
  309.3 1.1 fusion.95
  310.4 1.1 fusion.96
  311.8 1.1 fusion.97
  314.5 1.1 fusion.95
  315.6 1.1 fusion.96
  316.9 1.1 fusion.97
  319.9 39.4 %all-reduce = f32[544]{0:T(1024)S(1)} all-reduce(f32[544]{0:T(1024)S(1)} %maximum_dynamic-update-slice_fusion), channel_id=3, replica_groups=mesh['grp'=4,'dev'=8] {'grp','dev'}, use_global_device_ids=true, to_apply=%add | all-reduce | flops 544 | bytes 4352
  (112 shorter events, 40.9 us)
Async XLA Ops:
  7.2 82.1 %copy-start = (bf16[1,200,200]{2,1,0:T(8,128)(2,1)S(1)}, bf16[1,200,200]{2,1,0:T(8,128)(2,1)}, u32[]{:S(2)}) copy-start(bf16[1,200,200]{2,1,0:T(8,128)(2,1)} %param.14) | copy-start | bytes 240004
  7.2 141.6 %reduce-scatter.2.cloned.1.call-start = ((), (), s32[]{:S(2)}) async-start(), calls=%async_computation.1 | async-start | bytes 921600 | tf_op jit(solution)/shard_map/reduce_scatter | solution.py:67
  8.3 11.1 %collective-permute-start = (bf16[1,200,200]{2,0,1:T(2,128)(2,1)S(1)}, bf16[1,200,200]{2,0,1:T(2,128)(2,1)S(1)}, u32[]{:S(2)}, u32[]{:S(2)}) collective-permute-start(bf16[1,200,200]{2,0,1:T(2,128)(2,1)S(1)} %copy.67), channel_id=1, source_target_pairs={{0,1},{1,2},{2,3},{3,4},{4,5},{5,6},{6,7},{7,0},{8,9},{9,10},{10,1... | collective-permute-start | bytes 240008 | tf_op jit(solution)/shard_map/ppermute | solution.py:19
  19.4 8.9 %collective-permute-start.1 = (bf16[1,200,200]{2,0,1:T(2,128)(2,1)S(1)}, bf16[1,200,200]{2,0,1:T(2,128)(2,1)S(1)}, u32[]{:S(2)}, u32[]{:S(2)}) collective-permute-start(bf16[1,200,200]{2,0,1:T(2,128)(2,1)S(1)} %collective-permute-done), channel_id=1, source_target_pairs={{0,1},{1,2},{2,3},{3,4},{4,5},{5,6},{6,7},{7,0},{8,9},{9,10},{10,1... | collective-permute-start | bytes 240008 | tf_op jit(solution)/shard_map/ppermute | solution.py:19
  28.4 8.5 %collective-permute-start.2 = (bf16[1,200,200]{2,0,1:T(2,128)(2,1)S(1)}, bf16[1,200,200]{2,0,1:T(2,128)(2,1)S(1)}, u32[]{:S(2)}, u32[]{:S(2)}) collective-permute-start(bf16[1,200,200]{2,0,1:T(2,128)(2,1)S(1)} %collective-permute-done.1), channel_id=1, source_target_pairs={{0,1},{1,2},{2,3},{3,4},{4,5},{5,6},{6,7},{7,0},{8,9},{9,10},{10,1... | collective-permute-start | bytes 240008 | tf_op jit(solution)/shard_map/ppermute | solution.py:19
  36.8 8.6 %collective-permute-start.3 = (bf16[1,200,200]{2,0,1:T(2,128)(2,1)S(1)}, bf16[1,200,200]{2,0,1:T(2,128)(2,1)}, u32[]{:S(2)}, u32[]{:S(2)}) collective-permute-start(bf16[1,200,200]{2,0,1:T(2,128)(2,1)S(1)} %collective-permute-done.2), channel_id=1, source_target_pairs={{0,1},{1,2},{2,3},{3,4},{4,5},{5,6},{6,7},{7,0},{8,9},{9,10},{10,1... | collective-permute-start | bytes 240008 | tf_op jit(solution)/shard_map/ppermute | solution.py:19
  45.4 8.7 %collective-permute-start.4 = (bf16[1,200,200]{2,0,1:T(2,128)(2,1)}, bf16[1,200,200]{2,0,1:T(2,128)(2,1)S(1)}, u32[]{:S(2)}, u32[]{:S(2)}) collective-permute-start(bf16[1,200,200]{2,0,1:T(2,128)(2,1)} %collective-permute-done.3), channel_id=1, source_target_pairs={{0,1},{1,2},{2,3},{3,4},{4,5},{5,6},{6,7},{7,0},{8,9},{9,10},{10,1... | collective-permute-start | bytes 240008 | tf_op jit(solution)/shard_map/ppermute | solution.py:19
  54.0 0.7 copy-start.3
  54.7 9.1 %collective-permute-start.5 = (bf16[1,200,200]{2,0,1:T(2,128)(2,1)S(1)}, bf16[1,200,200]{2,0,1:T(2,128)(2,1)}, u32[]{:S(2)}, u32[]{:S(2)}) collective-permute-start(bf16[1,200,200]{2,0,1:T(2,128)(2,1)S(1)} %collective-permute-done.4), channel_id=1, source_target_pairs={{0,1},{1,2},{2,3},{3,4},{4,5},{5,6},{6,7},{7,0},{8,9},{9,10},{10,1... | collective-permute-start | bytes 240008 | tf_op jit(solution)/shard_map/ppermute | solution.py:19
  63.9 9.0 %collective-permute-start.6 = (bf16[1,200,200]{2,0,1:T(2,128)(2,1)}, bf16[1,200,200]{2,0,1:T(2,128)(2,1)}, u32[]{:S(2)}, u32[]{:S(2)}) collective-permute-start(bf16[1,200,200]{2,0,1:T(2,128)(2,1)} %collective-permute-done.5), channel_id=1, source_target_pairs={{0,1},{1,2},{2,3},{3,4},{4,5},{5,6},{6,7},{7,0},{8,9},{9,10},{10,1... | collective-permute-start | bytes 240008 | tf_op jit(solution)/shard_map/ppermute | solution.py:19
  72.8 11.1 %copy-start.1 = (bf16[24,200,200]{2,1,0:T(8,128)(2,1)S(1)}, bf16[24,200,200]{2,1,0:T(8,128)(2,1)}, u32[]{:S(2)}) copy-start(bf16[24,200,200]{2,1,0:T(8,128)(2,1)} %param.13) | copy-start | bytes 5760004
  88.1 1.2 copy-start.2
  88.1 60.6 %copy-start.4 = (bf16[1,200,200]{2,1,0:T(8,128)(2,1)S(1)}, bf16[1,200,200]{2,1,0:T(8,128)(2,1)}, u32[]{:S(2)}) copy-start(bf16[1,200,200]{2,1,0:T(8,128)(2,1)} %param.12) | copy-start | bytes 240004
  88.1 60.6 %copy-start.5 = (bf16[1,200,200]{2,1,0:T(8,128)(2,1)S(1)}, bf16[1,200,200]{2,1,0:T(8,128)(2,1)}, u32[]{:S(2)}) copy-start(bf16[1,200,200]{2,1,0:T(8,128)(2,1)} %param.11) | copy-start | bytes 240004
  89.2 116.3 %copy-start.6 = (s32[384,2]{0,1:T(2,128)S(1)}, s32[384,2]{0,1:T(2,128)}, u32[]{:S(2)}) copy-start(s32[384,2]{0,1:T(2,128)} %param.15) | copy-start | bytes 9220
  89.2 116.3 %copy-start.7 = (s32[32]{0:T(128)S(1)}, s32[32]{0:T(128)}, u32[]{:S(2)}) copy-start(s32[32]{0:T(128)} %param.17) | copy-start | bytes 388
  89.2 115.1 %all-gather.4.cloned.1.call-start = ((), (), s32[]{:S(2)}) async-start(), calls=%async_computation.2 | async-start | bytes 2764800 | tf_op jit(solution)/shard_map/all_gather | solution.py:89
  204.4 27.7 %collective-permute-start.7 = (bf16[8,3,200,200]{3,2,1,0:T(8,128)(2,1)}, bf16[8,3,200,200]{3,2,1,0:T(8,128)(2,1)S(1)}, u32[]{:S(2)}, u32[]{:S(2)}) collective-permute-start(bf16[8,3,200,200]{3,2,1,0:T(8,128)(2,1)} %bitcast.125), channel_id=1, source_target_pairs={{0,24},{8,0},{16,8},{24,16},{1,25},{9,1},{17,9},{25,17},{2,26},{10... | collective-permute-start | bytes 5760008 | tf_op jit(solution)/shard_map/ppermute | solution.py:91
Sparse Core Ops, SparseCore 0:
  89.4 59.3 reduce-scatter.1
  152.5 51.7 all-gather.3
